TPU v7x, 512 devices: a whole 4x8x8 slice. The times are simulated.
512 devices in a mesh: seq: 32 (over x, y), dp: 8 (over z), domain: 2 (over core).
Axes of the slice: x: 4, y: 8, z: 8, core: 2. Of those that a mesh axis runs over, the one named last changes fastest.
Arguments:
- history: bfloat16 [2, 8, 8192, 1024], P('domain', 'dp', 'seq'), may hold values from -6 to 6
- qkv_weight: bfloat16 [2, 1024, 3072], P('domain', 'seq'), may hold values from -0.375 to 0.375
- norm_gain: float32 [2, 1024], P('domain'), may hold values from 0.1 to 1.9
- pool_gain: float32 [2, 1024], P('domain'), may hold values from 0.1 to 1.9
- lengths: int32 [2, 8], P('domain', 'dp'), may hold values from 1024 to 8192, as said below
- positives: int32 [8], replicated, may hold values from 0 to 7, each once
Outputs:
- user_vec: bfloat16 [2, 8, 1024], P('domain', 'dp', 'seq')
- loss: float32 [2, 8], P('domain', 'dp')
Inputs may be any that keep to these rules, and one draw needn't show every extreme that they name: `lengths`: in each domain one user has exactly 8192 valid events and another exactly 1024. `positives`: each user of the second domain is named exactly once.
All inputs are finite; a program needn't handle non-finite values.
Results may differ from a plain program's by a relative error of at most 0.0085.
Values may be sent and summed in bfloat16 or wider, within the bound.
A program may use at most 64 MiB of HBM per device.

v0:
```python
import jax
import jax.numpy as jnp
from jax import lax
from jax.sharding import PartitionSpec as P

HEADS = 8
HEAD_DIM = 128
logit_scale = 20.0
epsilon = 1e-06
highest = lax.Precision.HIGHEST


def carried_in(part, axis, combine, identity):
    place = lax.axis_index(axis)
    gathered = jax.tree.map(lambda a: lax.all_gather(a, axis), part)
    state = jax.tree.map(lambda a, e: jnp.zeros_like(a) + jnp.asarray(e, a.dtype), part, identity)

    def one(hop, state):
        return combine(
            state, jax.tree.map(lambda a: lax.dynamic_index_in_dim(a, hop, 0, False), gathered)
        )

    return lax.fori_loop(0, place, one, state)


def partner_2(block, axis, stride):
    count = lax.axis_size(axis)
    route = []
    for low in range(count):
        high = low | 1 << stride
        if high != low and high < count:
            route += [(low, high), (high, low)]
    return lax.ppermute(block, axis, route)


def feature_map(values):
    return jax.nn.elu(values) + 1.0


def add_pair(earlier, later):
    return (earlier[0] + later[0], earlier[1] + later[1])


def shards(history, qkv_weight, norm_gain, pool_gain, lengths, positives):
    seq_count = lax.axis_size("seq")
    seq_place = lax.axis_index("seq")
    group_place = lax.axis_index("dp")
    domain_place = lax.axis_index("domain")
    events = history[0]
    users_dev, tokens_dev, width = events.shape
    row_count = users_dev * tokens_dev
    wide = events.astype(jnp.float32)
    normed = (
        wide * lax.rsqrt(jnp.mean(wide * wide, -1, keepdims=True) + epsilon) * norm_gain[0]
    ).astype(jnp.bfloat16)
    normed = normed.reshape(row_count, width)
    rows_here = qkv_weight[0]

    def add_rows(piece):
        return jnp.dot(normed, piece, preferred_element_type=jnp.float32)

    query_raw = add_rows(lax.all_gather(rows_here[:, :width], "seq", axis=0, tiled=True))
    key_raw = add_rows(lax.all_gather(rows_here[:, width : 2 * width], "seq", axis=0, tiled=True))
    value_raw = add_rows(lax.all_gather(rows_here[:, 2 * width :], "seq", axis=0, tiled=True))
    positions = seq_place * tokens_dev + jnp.arange(tokens_dev)
    valid = positions[None, :] < lengths[0][:, None]
    shape_heads = (users_dev, tokens_dev, HEADS, HEAD_DIM)
    queries = feature_map(query_raw).astype(jnp.bfloat16).reshape(shape_heads)
    key_feats = (
        jnp.where(valid.reshape(row_count)[:, None], feature_map(key_raw), 0.0)
        .astype(jnp.bfloat16)
        .reshape(shape_heads)
    )
    val_feats = value_raw.astype(jnp.bfloat16).reshape(shape_heads)
    local_state = jnp.einsum(
        "uthc,uthd->uhcd", key_feats, val_feats, preferred_element_type=jnp.float32
    )
    local_total = jnp.sum(key_feats.astype(jnp.float32), axis=1)
    state_before, total_before = carried_in(
        (local_state, local_total),
        "seq",
        add_pair,
        (jnp.zeros_like(local_state), jnp.zeros_like(local_total)),
    )
    causal = jnp.arange(tokens_dev)[:, None] >= jnp.arange(tokens_dev)[None, :]
    scores = jnp.einsum("uthc,ushc->uhts", queries, key_feats, preferred_element_type=jnp.float32)
    scores = jnp.where(causal, scores, 0.0)
    denominator = jnp.sum(scores, axis=-1) + jnp.einsum(
        "uthc,uhc->uht", queries.astype(jnp.float32), total_before, precision=highest
    )
    numerator = jnp.einsum(
        "uhts,ushc->uthc",
        scores.astype(jnp.bfloat16),
        val_feats,
        preferred_element_type=jnp.float32,
    )
    numerator = numerator + jnp.einsum(
        "uthc,uhcd->uthd",
        queries,
        state_before.astype(jnp.bfloat16),
        preferred_element_type=jnp.float32,
    )
    attended = numerator / jnp.transpose(denominator, (0, 2, 1))[..., None]
    attended = attended.reshape(users_dev, tokens_dev, width)
    partial_value = jnp.sum(jnp.where(valid[..., None], wide + attended, 0.0), axis=1)
    piece_width = width // seq_count
    gain_row = pool_gain[0]
    pooled = lax.psum(partial_value, "seq")
    factor = lax.rsqrt(jnp.mean(pooled * pooled, -1, keepdims=True) + epsilon)
    full_vec = (pooled * factor * gain_row).astype(jnp.bfloat16)
    out_vec = lax.dynamic_slice_in_dim(full_vec, seq_place * piece_width, piece_width, 1)
    group = lax.all_gather(full_vec, "dp", axis=0, tiled=True)
    other = partner_2(group, "domain", 0)
    logits = jnp.einsum("uc,vc->uv", full_vec, other, preferred_element_type=jnp.float32) * (
        logit_scale / width
    )
    users_all = other.shape[0]
    own_index = group_place * users_dev + jnp.arange(users_dev)
    targets = lax.dynamic_slice_in_dim(positives, group_place * users_dev, users_dev)
    forward_pair = targets[:, None] == jnp.arange(users_all)[None, :]
    backward_pair = positives[None, :] == own_index[:, None]
    partner = jnp.where(domain_place == 0, forward_pair, backward_pair)
    loss = jnp.log(jnp.sum(jnp.exp(logits), axis=-1)) - jnp.sum(
        jnp.where(partner, logits, 0.0), axis=-1
    )
    return (out_vec[None], loss[None])


def solution(mesh):
    placed = (
        P("domain", "dp", "seq", None),
        P("domain", "seq", None),
        P("domain", None),
        P("domain", None),
        P("domain", "dp"),
        P(),
    )
    return jax.shard_map(
        shards,
        mesh=mesh,
        in_specs=placed,
        out_specs=(P("domain", "dp", "seq"), P("domain", "dp")),
        check_vma=False,
    )
```

profile of v0, /device:TPU:1, one launch (start us, length us, event | category | flops | bytes accessed | tf_op | source)
XLA Modules:
  0.0 566.4 jit_solution(12575679889314143297)
XLA Ops:
  7.2 0.0 all-gather.11.cloned.1.call-start
  7.2 1.6 fusion.51
  8.8 0.0 all-gather.11.cloned.1.call-update
  8.8 0.0 all-gather.7.cloned.1.call-start
  8.9 0.7 all-gather.7.cloned.1.call-update
  9.6 0.0 all-gather.9.cloned.1.call-start
  9.6 0.7 all-gather.9.cloned.1.call-update
  10.3 0.0 all-gather.13.cloned.1.call-start
  11.0 1.2 fusion.5
  12.2 82.9 %all-gather.11.cloned.1.call-done = bf16[1024,1024]{1,0:T(8,128)(2,1)} async-done(((bf16[32,1024]{1,0:T(8,128)(2,1)}), bf16[1024,1024]{1,0:T(8,128)(2,1)}) %all-gather.11.cloned.1.call-update) | async-done | bytes 2097168 | tf_op jit(solution)/shard_map/all_gather | solution.py:63
  95.1 0.0 copy-start
  95.1 0.0 copy-start.2
  95.1 3.0 convert_reduce_fusion
  98.1 0.2 copy.43
  98.3 0.0 copy-start.3
  98.3 80.6 %all-gather.7.cloned.1.call-done = bf16[1024,1024]{1,0:T(8,128)(2,1)} async-done(((bf16[32,1024]{1,0:T(8,128)(2,1)}), bf16[1024,1024]{1,0:T(8,128)(2,1)}) %all-gather.7.cloned.1.call-update) | async-done | bytes 2097168 | tf_op jit(solution)/shard_map/all_gather | solution.py:64
  178.9 0.0 copy-done
  178.9 0.0 copy-done.2
  178.9 2.4 fusion.3
  181.3 1.1 fusion.29
  182.4 0.0 all-gather.13.cloned.1.call-update
  182.4 0.0 copy-done.3
  182.4 0.7 dynamic_slice.15
  183.1 31.5 %all_gather.30 = f32[32,1,8,128]{3,2,1,0:T(8,128)S(1)} all-gather(f32[1,1,8,128]{3,2,1,0:T(8,128)S(1)} %bitcast.122), channel_id=1, replica_groups=mesh['seq'=32,'dp'=8,'domain'=2] {'seq'}, dimensions={0}, use_global_device_ids=true | all-gather | bytes 135168 | tf_op jit(solution)/shard_map/all_gather | solution.py:15
  214.6 48.1 %all-gather.9.cloned.1.call-done = bf16[1024,1024]{1,0:T(8,128)(2,1)} async-done(((bf16[32,1024]{1,0:T(8,128)(2,1)}), bf16[1024,1024]{1,0:T(8,128)(2,1)}) %all-gather.9.cloned.1.call-update) | async-done | bytes 2097168 | tf_op jit(solution)/shard_map/all_gather | solution.py:62
  262.7 2.7 fusion.22
  265.4 0.0 copy-start.4
  265.4 0.5 select_reduce_fusion
  266.0 0.4 fusion.11
  266.3 145.7 %all-gather.13.cloned.1.call-done = f32[256,128,128]{2,1,0:T(8,128)} async-done(((f32[8,128,128]{2,1,0:T(8,128)}), f32[256,128,128]{2,1,0:T(8,128)}) %all-gather.13.cloned.1.call-update) | async-done | bytes 16777232 | tf_op jit(solution)/shard_map/all_gather | solution.py:15
  412.1 0.0 copy-done.4
  412.1 0.5 fusion.24
  412.6 1.4 fusion.21
  414.0 0.0 copy-start.1
  414.0 0.3 copy.37
  414.3 0.2 fusion.7
  414.6 94.9 %psum.7 = f32[1,1024]{1,0:T(1,128)S(1)} all-reduce(f32[1,1024]{1,0:T(1,128)S(1)} %bitcast.119), channel_id=1, replica_groups=mesh['seq'=32,'dp'=8,'domain'=2] {'seq'}, use_global_device_ids=true, to_apply=%region_6.7 | all-reduce | flops 1024 | bytes 8192 | tf_op jit(solution)/shard_map/psum | solution.py:108
  509.5 0.6 multiply_reduce_fusion
  510.8 0.0 copy-done.1
  510.8 20.9 %all-gather.1 = bf16[8,1,1024]{2,1,0:T(2,128)(2,1)S(1)} all-gather(bf16[1,1,1024]{2,1,0:T(2,128)(2,1)S(1)} %bitcast.121), channel_id=1, replica_groups=mesh['seq'=32,'dp'=8,'domain'=2] {'dp'}, dimensions={0}, use_global_device_ids=true | all-gather | bytes 18432 | tf_op jit(solution)/shard_map/all_gather | solution.py:112
  531.7 23.3 %collective-permute-start = (bf16[8,1024]{1,0:T(8,128)(2,1)S(1)}, bf16[8,1024]{1,0:T(8,128)(2,1)S(1)}, u32[]{:S(2)}, u32[]{:S(2)}) collective-permute-start(bf16[8,1024]{1,0:T(8,128)(2,1)S(1)} %bitcast.120), channel_id=1, source_target_pairs={{0,1},{1,0},{2,3},{3,2},{4,5},{5,4},{6,7},{7,6},{8,9},{9,8},{10,11... | collective-permute-start | bytes 49160 | tf_op jit(solution)/shard_map/ppermute | solution.py:33
  555.0 0.6 dynamic-slice_bitcast_fusion
  555.6 0.2 collective-permute-done
  555.8 1.5 fusion.40
  (9 shorter events, 0.1 us)
Async XLA Ops:
  7.2 87.9 %all-gather.11.cloned.1.call-start = ((), (), s32[]{:S(2)}) async-start(), calls=%async_computation.2 | async-start | bytes 2162688 | tf_op jit(solution)/shard_map/all_gather | solution.py:63
  8.8 170.1 %all-gather.7.cloned.1.call-start = ((), (), s32[]{:S(2)}) async-start(), calls=%async_computation | async-start | bytes 2162688 | tf_op jit(solution)/shard_map/all_gather | solution.py:64
  9.6 253.1 %all-gather.9.cloned.1.call-start = ((), (), s32[]{:S(2)}) async-start(), calls=%async_computation.1 | async-start | bytes 2162688 | tf_op jit(solution)/shard_map/all_gather | solution.py:62
  10.3 401.7 %all-gather.13.cloned.1.call-start = ((), (), s32[]{:S(2)}) async-start(), calls=%async_computation.3 | async-start | bytes 17301504 | tf_op jit(solution)/shard_map/all_gather | solution.py:15
  95.1 83.8 %copy-start = (bf16[1,1,256,1024]{3,2,1,0:T(8,128)(2,1)S(1)}, bf16[1,1,256,1024]{3,2,1,0:T(8,128)(2,1)}, u32[]{:S(2)}) copy-start(bf16[1,1,256,1024]{3,2,1,0:T(8,128)(2,1)} %param.8) | copy-start | bytes 1572868
  95.1 83.8 %copy-start.2 = (f32[1,1024]{1,0:T(1,128)S(1)}, f32[1,1024]{1,0:T(1,128)}, u32[]{:S(2)}) copy-start(f32[1,1024]{1,0:T(1,128)} %param.10) | copy-start | bytes 12292
  98.3 84.1 %copy-start.3 = (s32[8]{0:T(128)S(1)}, s32[8]{0:T(128)}, u32[]{:S(2)}) copy-start(s32[8]{0:T(128)} %param.13) | copy-start | bytes 100
  265.4 146.6 %copy-start.4 = (bf16[32,8,8,128]{3,2,1,0:T(8,128)(2,1)}, bf16[32,8,8,128]{3,2,1,0:T(8,128)(2,1)S(1)}, u32[]{:S(2)}) copy-start(bf16[32,8,8,128]{3,2,1,0:T(8,128)(2,1)S(1)} %fusion.22) | copy-start | bytes 1572868
  414.0 96.8 %copy-start.1 = (f32[1,1024]{1,0:T(1,128)S(1)}, f32[1,1024]{1,0:T(1,128)}, u32[]{:S(2)}) copy-start(f32[1,1024]{1,0:T(1,128)} %param.11) | copy-start | bytes 12292
  531.7 24.1 %collective-permute-start = (bf16[8,1024]{1,0:T(8,128)(2,1)S(1)}, bf16[8,1024]{1,0:T(8,128)(2,1)S(1)}, u32[]{:S(2)}, u32[]{:S(2)}) collective-permute-start(bf16[8,1024]{1,0:T(8,128)(2,1)S(1)} %bitcast.120), channel_id=1, source_target_pairs={{0,1},{1,0},{2,3},{3,2},{4,5},{5,4},{6,7},{7,6},{8,9},{9,8},{10,11... | collective-permute-start | bytes 49160 | tf_op jit(solution)/shard_map/ppermute | solution.py:33
Sparse Core Ops, SparseCore 0:
  11.1 83.9 all-gather.10
  98.3 80.6 all-gather.6
  182.1 80.5 all-gather.8
  265.7 146.2 all-gather.12
where the time goes:
time: 568 us; the launch traced here: 566 us
  waiting for transfers between devices  359 us (63%)
  blocking collectives  147 us (26%)
  starting transfers between devices  23.4 us (4%)
  between operations  17.8 us (3%)
  matrix products  13.5 us (2%)
    all_gather x1, waiting for transfers between devices, carried_in(): gathered = jax.tree.map(lambda a: lax.all_gather(a, axis), part)  146 us
    psum x1, blocking collectives, shards(): pooled = lax.psum(partial_value, 'seq')  94.9 us
    all_gather x1, waiting for transfers between devices, shards(): lax.all_gather(rows_here[:, width:2 * width], 'seq', axis=0, tiled=True)  82.9 us
    all_gather x1, waiting for transfers between devices, shards(): lax.all_gather(rows_here[:, 2 * width:], 'seq', axis=0, tiled=True)  80.6 us
    all_gather x1, waiting for transfers between devices, shards(): lax.all_gather(rows_here[:, :width], 'seq', axis=0, tiled=True)  48.1 us
    all_gather x1, blocking collectives, carried_in(): gathered = jax.tree.map(lambda a: lax.all_gather(a, axis), part)  31.5 us
    ppermute x1, starting transfers between devices, partner_2(): return lax.ppermute(block, axis, route)  23.3 us
    all_gather x1, blocking collectives, shards(): group = lax.all_gather(full_vec, 'dp', axis=0, tiled=True)  20.9 us
  transfers between devices with their start and end apart: 5, of which 5 were waited for; matrix products, arithmetic and copies ran while one was open for 2% of the time, Pallas kernels for 0%

commit v1 on v0

--- a/solution.py
+++ b/solution.py
@@ -1,3 +1,4 @@
+import functools
 import jax
 import jax.numpy as jnp
 from jax import lax
@@ -8,6 +9,15 @@
 logit_scale = 20.0
 epsilon = 1e-06
 highest = lax.Precision.HIGHEST
+
+
+def trace_heaps(sheet, group_axis):
+    return jnp.concatenate(
+        lax.all_to_all(jnp.stack([sheet] * lax.axis_size(group_axis)), group_axis, 0, 0), axis=0
+    )
+
+
+mix_the_vector = functools.partial(trace_heaps, group_axis="seq")
 
 
 def carried_in(part, axis, combine, identity):
@@ -60,7 +70,7 @@
         return jnp.dot(normed, piece, preferred_element_type=jnp.float32)
 
     query_raw = add_rows(lax.all_gather(rows_here[:, :width], "seq", axis=0, tiled=True))
-    key_raw = add_rows(lax.all_gather(rows_here[:, width : 2 * width], "seq", axis=0, tiled=True))
+    key_raw = add_rows(mix_the_vector(rows_here[:, width : 2 * width]))
     value_raw = add_rows(lax.all_gather(rows_here[:, 2 * width :], "seq", axis=0, tiled=True))
     positions = seq_place * tokens_dev + jnp.arange(tokens_dev)
     valid = positions[None, :] < lengths[0][:, None]

time: 568 us -> 490 us (0.86)
  waiting for transfers between devices: 359 us -> 272 us
  starting transfers between devices: 23.4 us -> 34 us
    all_gather x1 -> x0, waiting for transfers between devices: 82.9 us -> none  [shards(): lax.all_gather(rows_here[:, width:2 * width], 'seq', axis=0, tiled=True)]
    all_gather x1, waiting for transfers between devices: 80.6 us -> 26.8 us  [shards(): lax.all_gather(rows_here[:, 2 * width:], 'seq', axis=0, tiled=True)]
    all_to_all x0 -> x1, waiting for transfers between devices: none -> 50 us  [trace_heaps(): lax.all_to_all(jnp.stack([sheet] * lax.axis_size(group_axis)), group_axis...]
    all_to_all x0 -> x1, starting transfers between devices: none -> 10.6 us  [trace_heaps(): lax.all_to_all(jnp.stack([sheet] * lax.axis_size(group_axis)), group_axis...]
where the time goes in v1:
time: 490 us; the launch traced here: 489 us
  waiting for transfers between devices  272 us (56%)
  blocking collectives  147 us (30%)
  starting transfers between devices  34 us (7%)
  between operations  17.8 us (4%)
  matrix products  11.6 us (2%)
  local copies, waits for them, and re-layouts  4.97 us (1%)
    all_gather x1, waiting for transfers between devices, carried_in(): gathered = jax.tree.map(lambda a: lax.all_gather(a, axis), part)  146 us
    psum x1, blocking collectives, shards(): pooled = lax.psum(partial_value, 'seq')  94.8 us
    all_to_all x1, waiting for transfers between devices, trace_heaps(): lax.all_to_all(jnp.stack([sheet] * lax.axis_size(group_axis)), group_axis...  50 us
    all_gather x1, waiting for transfers between devices, shards(): lax.all_gather(rows_here[:, :width], 'seq', axis=0, tiled=True)  48.2 us
    all_gather x1, blocking collectives, carried_in(): gathered = jax.tree.map(lambda a: lax.all_gather(a, axis), part)  31.7 us
    all_gather x1, waiting for transfers between devices, shards(): lax.all_gather(rows_here[:, 2 * width:], 'seq', axis=0, tiled=True)  26.8 us
    ppermute x1, starting transfers between devices, partner_2(): return lax.ppermute(block, axis, route)  23.3 us
    all_gather x1, blocking collectives, shards(): group = lax.all_gather(full_vec, 'dp', axis=0, tiled=True)  20.9 us
  transfers between devices with their start and end apart: 5, of which 5 were waited for; matrix products, arithmetic and copies ran while one was open for 2% of the time, Pallas kernels for 0%

profile of v1, /device:TPU:1, one launch (start us, length us, event | category | flops | bytes accessed | tf_op | source)
XLA Modules:
  0.0 488.6 jit_solution(4531365489495566197)
XLA Ops:
  7.2 0.0 all-gather.6.cloned.1.call-start
  7.2 1.6 fusion.56
  8.8 0.0 all-gather.6.cloned.1.call-update
  8.8 1.6 stack.2
  10.3 0.0 copy-start
  10.3 0.0 copy-start.2
  10.4 10.6 %all-to-all-start = ((bf16[32,32,1024]{2,1,0:T(8,128)(2,1)}), bf16[32,32,1024]{2,1,0:T(8,128)(2,1)S(1)}, u32[]{:S(2)}, u32[]{:S(2)}) async-start(bf16[32,32,1024]{2,1,0:T(8,128)(2,1)} %stack.2), calls=%async_computation | async-start | bytes 4194304 | tf_op jit(solution)/shard_map/all_to_all | solution.py:16
  21.0 0.0 all-gather.8.cloned.1.call-start
  21.0 0.7 all-gather.8.cloned.1.call-update
  21.7 0.0 all-gather.10.cloned.1.call-start
  22.4 0.0 copy-done
  22.5 0.2 fusion.5
  22.6 50.0 %all-to-all-done = bf16[32,32,1024]{2,1,0:T(8,128)(2,1)S(1)} async-done(((bf16[32,32,1024]{2,1,0:T(8,128)(2,1)}), bf16[32,32,1024]{2,1,0:T(8,128)(2,1)S(1)}, u32[]{:S(2)}, u32[]{:S(2)}) %all-to-all-start) | async-done | bytes 2097184 | tf_op jit(solution)/shard_map/all_to_all | solution.py:16
  72.7 0.0 copy-done.2
  72.7 1.2 convert_reduce_fusion
  73.9 0.2 copy.43
  74.1 0.0 copy-start.3
  74.1 26.8 %all-gather.6.cloned.1.call-done = bf16[1024,1024]{1,0:T(8,128)(2,1)} async-done(((bf16[32,1024]{1,0:T(8,128)(2,1)}), bf16[1024,1024]{1,0:T(8,128)(2,1)}) %all-gather.6.cloned.1.call-update) | async-done | bytes 2097168 | tf_op jit(solution)/shard_map/all_gather | solution.py:74
  100.9 2.3 fusion.3
  103.2 1.1 fusion.36
  104.3 0.0 all-gather.10.cloned.1.call-update
  104.4 0.0 copy-done.3
  104.4 0.7 dynamic_slice.15
  105.1 31.7 %all_gather.26 = f32[32,1,8,128]{3,2,1,0:T(8,128)S(1)} all-gather(f32[1,1,8,128]{3,2,1,0:T(8,128)S(1)} %bitcast.126), channel_id=1, replica_groups=mesh['seq'=32,'dp'=8,'domain'=2] {'seq'}, dimensions={0}, use_global_device_ids=true | all-gather | bytes 135168 | tf_op jit(solution)/shard_map/all_gather | solution.py:25
  136.7 48.2 %all-gather.8.cloned.1.call-done = bf16[1024,1024]{1,0:T(8,128)(2,1)} async-done(((bf16[32,1024]{1,0:T(8,128)(2,1)}), bf16[1024,1024]{1,0:T(8,128)(2,1)}) %all-gather.8.cloned.1.call-update) | async-done | bytes 2097168 | tf_op jit(solution)/shard_map/all_gather | solution.py:72
  184.9 2.7 fusion.24
  187.6 0.0 copy-start.4
  187.6 0.5 select_reduce_fusion
  188.2 0.4 fusion.13
  188.5 145.8 %all-gather.10.cloned.1.call-done = f32[256,128,128]{2,1,0:T(8,128)} async-done(((f32[8,128,128]{2,1,0:T(8,128)}), f32[256,128,128]{2,1,0:T(8,128)}) %all-gather.10.cloned.1.call-update) | async-done | bytes 16777232 | tf_op jit(solution)/shard_map/all_gather | solution.py:25
  334.4 0.0 copy-done.4
  334.4 0.5 fusion.31
  334.9 1.4 fusion.23
  336.4 0.0 copy-start.1
  336.4 0.3 copy.37
  336.7 0.2 fusion.7
  336.9 94.8 %psum.7 = f32[1,1024]{1,0:T(1,128)S(1)} all-reduce(f32[1,1024]{1,0:T(1,128)S(1)} %bitcast.123), channel_id=1, replica_groups=mesh['seq'=32,'dp'=8,'domain'=2] {'seq'}, use_global_device_ids=true, to_apply=%region_6.7 | all-reduce | flops 1024 | bytes 8192 | tf_op jit(solution)/shard_map/psum | solution.py:118
  431.7 0.6 multiply_reduce_fusion
  433.0 0.0 copy-done.1
  433.0 20.9 %all-gather.1 = bf16[8,1,1024]{2,1,0:T(2,128)(2,1)S(1)} all-gather(bf16[1,1,1024]{2,1,0:T(2,128)(2,1)S(1)} %bitcast.125), channel_id=1, replica_groups=mesh['seq'=32,'dp'=8,'domain'=2] {'dp'}, dimensions={0}, use_global_device_ids=true | all-gather | bytes 18432 | tf_op jit(solution)/shard_map/all_gather | solution.py:122
  453.9 23.3 %collective-permute-start = (bf16[8,1024]{1,0:T(8,128)(2,1)S(1)}, bf16[8,1024]{1,0:T(8,128)(2,1)S(1)}, u32[]{:S(2)}, u32[]{:S(2)}) collective-permute-start(bf16[8,1024]{1,0:T(8,128)(2,1)S(1)} %bitcast.124), channel_id=1, source_target_pairs={{0,1},{1,0},{2,3},{3,2},{4,5},{5,4},{6,7},{7,6},{8,9},{9,8},{10,11... | collective-permute-start | bytes 49160 | tf_op jit(solution)/shard_map/ppermute | solution.py:43
  477.2 0.6 dynamic-slice_bitcast_fusion
  477.8 0.2 collective-permute-done
  478.0 1.5 fusion.54
  (9 shorter events, 0.1 us)
Async XLA Ops:
  7.2 93.7 %all-gather.6.cloned.1.call-start = ((), (), s32[]{:S(2)}) async-start(), calls=%async_computation.1 | async-start | bytes 2162688 | tf_op jit(solution)/shard_map/all_gather | solution.py:74
  10.3 12.1 %copy-start = (bf16[1,1,256,1024]{3,2,1,0:T(8,128)(2,1)S(1)}, bf16[1,1,256,1024]{3,2,1,0:T(8,128)(2,1)}, u32[]{:S(2)}) copy-start(bf16[1,1,256,1024]{3,2,1,0:T(8,128)(2,1)} %param.8) | copy-start | bytes 1572868
  10.3 62.3 %copy-start.2 = (f32[1,1024]{1,0:T(1,128)S(1)}, f32[1,1024]{1,0:T(1,128)}, u32[]{:S(2)}) copy-start(f32[1,1024]{1,0:T(1,128)} %param.10) | copy-start | bytes 12292
  10.4 62.3 %all-to-all-start = ((bf16[32,32,1024]{2,1,0:T(8,128)(2,1)}), bf16[32,32,1024]{2,1,0:T(8,128)(2,1)S(1)}, u32[]{:S(2)}, u32[]{:S(2)}) async-start(bf16[32,32,1024]{2,1,0:T(8,128)(2,1)} %stack.2), calls=%async_computation | async-start | bytes 4194304 | tf_op jit(solution)/shard_map/all_to_all | solution.py:16
  21.0 163.9 %all-gather.8.cloned.1.call-start = ((), (), s32[]{:S(2)}) async-start(), calls=%async_computation.2 | async-start | bytes 2162688 | tf_op jit(solution)/shard_map/all_gather | solution.py:72
  21.7 312.6 %all-gather.10.cloned.1.call-start = ((), (), s32[]{:S(2)}) async-start(), calls=%async_computation.3 | async-start | bytes 17301504 | tf_op jit(solution)/shard_map/all_gather | solution.py:25
  74.1 30.3 %copy-start.3 = (s32[8]{0:T(128)S(1)}, s32[8]{0:T(128)}, u32[]{:S(2)}) copy-start(s32[8]{0:T(128)} %param.13) | copy-start | bytes 100
  187.6 146.8 %copy-start.4 = (bf16[32,8,8,128]{3,2,1,0:T(8,128)(2,1)}, bf16[32,8,8,128]{3,2,1,0:T(8,128)(2,1)S(1)}, u32[]{:S(2)}) copy-start(bf16[32,8,8,128]{3,2,1,0:T(8,128)(2,1)S(1)} %fusion.24) | copy-start | bytes 1572868
  336.4 96.7 %copy-start.1 = (f32[1,1024]{1,0:T(1,128)S(1)}, f32[1,1024]{1,0:T(1,128)}, u32[]{:S(2)}) copy-start(f32[1,1024]{1,0:T(1,128)} %param.11) | copy-start | bytes 12292
  453.9 24.1 %collective-permute-start = (bf16[8,1024]{1,0:T(8,128)(2,1)S(1)}, bf16[8,1024]{1,0:T(8,128)(2,1)S(1)}, u32[]{:S(2)}, u32[]{:S(2)}) collective-permute-start(bf16[8,1024]{1,0:T(8,128)(2,1)S(1)} %bitcast.124), channel_id=1, source_target_pairs={{0,1},{1,0},{2,3},{3,2},{4,5},{5,4},{6,7},{7,6},{8,9},{9,8},{10,11... | collective-permute-start | bytes 49160 | tf_op jit(solution)/shard_map/ppermute | solution.py:43
Sparse Core Ops, SparseCore 0:
  11.1 89.7 all-gather.5
  104.1 80.7 all-gather.7
  188.1 146.2 all-gather.9
